TPU v7x, 128 devices: a whole 4x4x4 slice. The times are simulated.
128 devices in a mesh: dp: 16 (over y, x), head: 8 (over z, core).
Axes of the slice: x: 4, y: 4, z: 4, core: 2. Of those that a mesh axis runs over, the one named last changes fastest.
Arguments:
- slot_token_ids: int32 [128, 512], P('dp'), may hold values from 0 to 50264
- lengths: int32 [128], P('dp'), may hold values from 64 to 512, as said below
- labels: int32 [128], P('dp'), may hold values from 0 to 2
- optimizer_step_count: int32 [], replicated, may hold values from 2 to 20
- token_embedding_table: bfloat16 [50304, 1024], P('dp', 'head'), may hold values from -6 to 6
- positions: bfloat16 [512, 1024], replicated, may hold values from -4 to 4
- query_key_value_weight: bfloat16 [3, 1024, 1024], P(None, None, 'head'), may hold values from -0.1875 to 0.1875
- attention_output_weight: bfloat16 [1024, 1024], P('head'), may hold values from -0.8 to 0.8
- feedforward_input_weight: bfloat16 [1024, 4096], P(None, 'head'), may hold values from -0.1875 to 0.1875
- feedforward_output_weight: bfloat16 [4096, 1024], P('head'), may hold values from -0.09375 to 0.09375
- layer_norm_gains: float32 [3, 1024], replicated, may hold values from 0.5 to 1.5
- layer_norm_biases: float32 [3, 1024], replicated, may hold values from -2 to 2
- classifier: bfloat16 [3, 1024], replicated, may hold values from -0.75 to 0.75
- adapter_down_maps: float32 [2, 1024, 16], replicated, may hold values from -0.1875 to 0.1875
- adapter_up_maps: float32 [2, 16, 1024], P(None, None, 'head'), may hold values from -1.5 to 1.5
- down_first_moment: float32 [2, 1024, 16], P(None, 'dp'), may hold values from -0.0078125 to 0.0078125
- down_second_moment: float32 [2, 1024, 16], P(None, 'dp'), may hold values from 2.1972657e-08 to 9.1552735e-08
- up_first_moment: float32 [2, 16, 1024], P(None, None, ('head', 'dp')), may hold values from -0.0078125 to 0.0078125
- up_second_moment: float32 [2, 16, 1024], P(None, None, ('head', 'dp')), may hold values from 2.1972657e-08 to 9.1552735e-08
- down_privacy_noise: float32 [2, 1024, 16], P(None, 'dp'), may hold values from -6 to 6
- up_privacy_noise: float32 [2, 16, 1024], P(None, None, ('head', 'dp')), may hold values from -6 to 6
Outputs:
- loss: float32 [], replicated
- example_norms: float32 [128], P(('dp', 'head'))
- a_moment1: float32 [2, 1024, 16], P(None, 'dp')
- a_moment2: float32 [2, 1024, 16], P(None, 'dp')
- a_weight: float32 [2, 1024, 16], P(None, 'dp')
- b_moment1: float32 [2, 16, 1024], P(None, None, ('head', 'dp'))
- b_moment2: float32 [2, 16, 1024], P(None, None, ('head', 'dp'))
- b_weight: float32 [2, 16, 1024], P(None, None, ('head', 'dp'))
- lamb_norms: float32 [4, 2], replicated
Inputs may be any that keep to these rules, and one draw needn't show every extreme that they name: `lengths`: valid tokens of each example; some example has exactly 512.
All inputs are finite; a program needn't handle non-finite values.
Results may differ from a plain program's by a relative error of at most 0.0059.
Values may be sent and summed in bfloat16 or wider, within the bound.
No kernel may reach another device: no remote copies, remote signals or barrier semaphores. Data moves between devices by JAX's collectives and lax.ppermute only.
A program may use at most 256 MiB of HBM per device.

v0:
```python
import jax
import jax.numpy as jnp
from jax import lax
from jax.sharding import PartitionSpec as P

HDIM = 64
MICRO = 4
precise = lax.Precision.HIGHEST
adapter_scale = 2.0
clip_bound = 1.0
noise_mult = 0.6
smooth_rate = 0.1
beta_one = 0.9
beta_two = 0.999
adam_eps = 1e-06
decay_rate = 0.01
learn_rate = 0.25
norm_eps = 1e-05
contract_last = (((1,), (1,)), ((), ()))


def gelu_exact(inputs):
    return jax.nn.gelu(inputs, approximate=False)


def norm_rows(inputs, gain, bias):
    centre = inputs - jnp.mean(inputs, -1, keepdims=True)
    inv_std = lax.rsqrt(jnp.mean(centre * centre, -1, keepdims=True) + norm_eps)
    return (centre * inv_std * gain + bias, inv_std)


def norm_back(grad, normed, inv_std, gain, bias):
    x_hat = (normed - bias) / gain
    scaled = grad * gain
    return inv_std * (
        scaled
        - jnp.mean(scaled, -1, keepdims=True)
        - x_hat * jnp.mean(scaled * x_hat, -1, keepdims=True)
    )


def branch_add(partial_out, resid, gain, bias):
    total = lax.psum(partial_out, "head")
    return norm_rows(resid + total, gain, bias)


def masked_scores(query_h, key_h, valid_mask):
    scores = jnp.einsum(
        "eqhd,ekhd->ehqk", query_h, key_h, preferred_element_type=jnp.float32
    ) * HDIM ** (-0.5)
    return jnp.where(valid_mask[:, None, None, :], scores, -1e30)


def layer_forward(
    hidden_initial, valid_mask, length_float, class_label, frozen_params, adapter_reduced
):
    w_qkv, w_o, w_in, w_out, gains, biases, class_w = frozen_params
    down_pair, up_reduced = adapter_reduced
    example_count, sequence_length = valid_mask.shape
    width = hidden_initial.shape[1]
    local_w = w_o.shape[0]
    adapter_width = up_reduced.shape[1]
    shape4 = (example_count, sequence_length, local_w // HDIM, HDIM)
    hidden_reduced = hidden_initial.astype(jnp.bfloat16)
    adapter_activation = jnp.dot(
        hidden_reduced, down_pair, preferred_element_type=jnp.float32
    ).astype(jnp.bfloat16)
    query_low = (
        (
            jnp.dot(hidden_reduced, w_qkv[0], preferred_element_type=jnp.float32)
            + adapter_scale
            * jnp.dot(
                adapter_activation[:, :adapter_width],
                up_reduced[0],
                preferred_element_type=jnp.float32,
            )
        )
        .astype(jnp.bfloat16)
        .reshape(shape4)
    )
    key_low = (
        jnp.dot(hidden_reduced, w_qkv[1], preferred_element_type=jnp.float32)
        .astype(jnp.bfloat16)
        .reshape(shape4)
    )
    value_low = (
        (
            jnp.dot(hidden_reduced, w_qkv[2], preferred_element_type=jnp.float32)
            + adapter_scale
            * jnp.dot(
                adapter_activation[:, adapter_width:],
                up_reduced[1],
                preferred_element_type=jnp.float32,
            )
        )
        .astype(jnp.bfloat16)
        .reshape(shape4)
    )
    scores = masked_scores(query_low, key_low, valid_mask)
    row_top = jnp.max(scores, -1, keepdims=True)
    log_total = row_top + jnp.log(jnp.sum(jnp.exp(scores - row_top), -1, keepdims=True))
    attn_prob = jnp.exp(scores - log_total)
    context = (
        jnp.einsum(
            "ehqk,ekhd->eqhd",
            attn_prob.astype(jnp.bfloat16),
            value_low,
            preferred_element_type=jnp.float32,
        )
        .astype(jnp.bfloat16)
        .reshape(-1, local_w)
    )
    hidden_one, std_one = branch_add(
        jnp.dot(context, w_o, preferred_element_type=jnp.float32),
        hidden_initial,
        gains[1],
        biases[1],
    )
    ffn_pre = jnp.dot(hidden_one.astype(jnp.bfloat16), w_in, preferred_element_type=jnp.float32)
    ffn_part = jnp.dot(
        gelu_exact(ffn_pre).astype(jnp.bfloat16), w_out, preferred_element_type=jnp.float32
    )
    hidden_two, std_two = branch_add(ffn_part, hidden_one, gains[2], biases[2])
    valid_f = valid_mask.astype(jnp.float32)
    pooled = (
        jnp.sum(hidden_two.reshape(example_count, sequence_length, width) * valid_f[..., None], 1)
        / length_float[:, None]
    )
    logits = lax.dot_general(
        pooled.astype(jnp.bfloat16), class_w, contract_last, preferred_element_type=jnp.float32
    )
    log_prob = jax.nn.log_softmax(logits, -1)
    target = (1.0 - smooth_rate) * jax.nn.one_hot(
        class_label, class_w.shape[0], dtype=jnp.float32
    ) + smooth_rate / class_w.shape[0]
    losses = -jnp.sum(target * log_prob, -1)
    d_logit = jnp.exp(log_prob) - target
    d_pooled = jnp.dot(d_logit, class_w.astype(jnp.float32), precision=precise)
    d_two = (d_pooled[:, None, :] * (valid_f / length_float[:, None])[..., None]).reshape(-1, width)
    d_sum_two = norm_back(d_two, hidden_two, std_two, gains[2], biases[2])
    grad_act = lax.dot_general(
        d_sum_two.astype(jnp.bfloat16), w_out, contract_last, preferred_element_type=jnp.float32
    )
    d_pre = jax.vjp(gelu_exact, ffn_pre)[1](grad_act)[0].astype(jnp.bfloat16)
    back_part = lax.dot_general(d_pre, w_in, contract_last, preferred_element_type=jnp.float32)
    d_one = d_sum_two + lax.psum(back_part, "head")
    d_attn = norm_back(d_one, hidden_one, std_one, gains[1], biases[1]).astype(jnp.bfloat16)
    d_context = (
        lax.dot_general(d_attn, w_o, contract_last, preferred_element_type=jnp.float32)
        .astype(jnp.bfloat16)
        .reshape(shape4)
    )
    attn_prob = jnp.exp(masked_scores(query_low, key_low, valid_mask) - log_total)
    d_value = jnp.einsum(
        "ehqk,eqhd->ekhd",
        attn_prob.astype(jnp.bfloat16),
        d_context,
        preferred_element_type=jnp.float32,
    ).astype(jnp.bfloat16)
    d_prob = jnp.einsum("eqhd,ekhd->ehqk", d_context, value_low, preferred_element_type=jnp.float32)
    d_score = (attn_prob * (d_prob - jnp.sum(attn_prob * d_prob, -1, keepdims=True))).astype(
        jnp.bfloat16
    )
    d_query = (
        jnp.einsum("ehqk,ekhd->eqhd", d_score, key_low, preferred_element_type=jnp.float32)
        * HDIM ** (-0.5)
    ).astype(jnp.bfloat16)
    dq_rows = d_query.reshape(-1, local_w)
    dv_rows = d_value.reshape(-1, local_w)
    example_activation = adapter_activation.reshape(
        example_count, sequence_length, 2 * adapter_width
    )
    up_gradient = adapter_scale * jnp.stack(
        [
            jnp.einsum(
                "elr,eld->erd",
                example_activation[..., :adapter_width],
                dq_rows.reshape(example_count, sequence_length, local_w),
                preferred_element_type=jnp.float32,
            ),
            jnp.einsum(
                "elr,eld->erd",
                example_activation[..., adapter_width:],
                dv_rows.reshape(example_count, sequence_length, local_w),
                preferred_element_type=jnp.float32,
            ),
        ],
        1,
    )
    inner_portion = adapter_scale * jnp.concatenate(
        [
            lax.dot_general(
                dq_rows, up_reduced[0], contract_last, preferred_element_type=jnp.float32
            ),
            lax.dot_general(
                dv_rows, up_reduced[1], contract_last, preferred_element_type=jnp.float32
            ),
        ],
        1,
    )
    inner_full = lax.psum(inner_portion, "head")
    inner_sum = inner_full.astype(jnp.bfloat16)
    grad_both = jnp.einsum(
        "eld,elr->edr",
        hidden_reduced.reshape(example_count, sequence_length, width),
        inner_sum.reshape(example_count, sequence_length, 2 * adapter_width),
        preferred_element_type=jnp.float32,
    )
    down_gradient = jnp.stack([grad_both[..., :adapter_width], grad_both[..., adapter_width:]], 1)
    return (losses, down_gradient, up_gradient)


def apply_blocks(hidden_rows, lengths, labels, frozen_params, adapter_reduced, encoder_block):
    example_count, sequence_length, width = hidden_rows.shape
    valid_all = jnp.arange(sequence_length)[None, :] < lengths[:, None]
    loss_list, down_list, up_list = ([], [], [])
    for block_idx in range(example_count // encoder_block):
        first_ex = block_idx * encoder_block
        last_ex = first_ex + encoder_block
        losses, down_gradient, up_gradient = layer_forward(
            hidden_rows[first_ex:last_ex].reshape(-1, width),
            valid_all[first_ex:last_ex],
            lengths[first_ex:last_ex].astype(jnp.float32),
            labels[first_ex:last_ex],
            frozen_params,
            adapter_reduced,
        )
        loss_list.append(losses)
        down_list.append(down_gradient)
        up_list.append(up_gradient)
    return (
        jnp.concatenate(loss_list, 0),
        jnp.concatenate(down_list, 0),
        jnp.concatenate(up_list, 0),
    )


def lamb_direction(weight, grad, first, second, step_number):
    first_new = beta_one * first + (1.0 - beta_one) * grad
    second_new = beta_two * second + (1.0 - beta_two) * grad * grad
    direction = (
        first_new
        / (1.0 - jnp.power(beta_one, step_number))
        / (jnp.sqrt(second_new / (1.0 - jnp.power(beta_two, step_number))) + adam_eps)
        + decay_rate * weight
    )
    return (first_new, second_new, direction)


def per_device(
    slot_token_ids,
    lengths,
    labels,
    optimizer_step_count,
    token_embedding_table,
    positions,
    query_key_value_weight,
    attention_output_weight,
    feedforward_input_weight,
    feedforward_output_weight,
    layer_norm_gains,
    layer_norm_biases,
    classifier,
    adapter_down_maps,
    adapter_up_maps,
    down_first_moment,
    down_second_moment,
    up_first_moment,
    up_second_moment,
    down_privacy_noise,
    up_privacy_noise,
):
    n_head = lax.axis_size("head")
    dataset_size = lax.axis_size("dp")
    ex_dev, sequence_length = slot_token_ids.shape
    width = positions.shape[1]
    every_ids = lax.all_gather(slot_token_ids, "dp", axis=0, tiled=True).reshape(-1)
    vocab_local = token_embedding_table.shape[0]
    offset = lax.axis_index("dp") * vocab_local
    ids_here = every_ids - offset
    inside = (ids_here >= 0) & (ids_here < vocab_local)
    picked = jnp.take(token_embedding_table, jnp.clip(ids_here, 0, vocab_local - 1), axis=0)
    columns = lax.psum_scatter(
        jnp.where(inside[:, None], picked.astype(jnp.float32), 0.0).astype(jnp.bfloat16),
        "dp",
        scatter_dimension=0,
        tiled=True,
    )
    pos_f = positions.astype(jnp.float32)[None]
    down_reduced = adapter_down_maps.astype(jnp.bfloat16)
    down_pair = jnp.concatenate([down_reduced[0], down_reduced[1]], 1)
    micro_examples = ex_dev // MICRO
    own_share = ex_dev // n_head
    tokens = lax.all_gather(columns, "head", axis=1, tiled=True)
    hidden_all, unused_std = norm_rows(
        tokens.astype(jnp.float32).reshape(ex_dev, sequence_length, width) + pos_f,
        layer_norm_gains[0],
        layer_norm_biases[0],
    )
    frozen_params = (
        query_key_value_weight,
        attention_output_weight,
        feedforward_input_weight,
        feedforward_output_weight,
        layer_norm_gains,
        layer_norm_biases,
        classifier,
    )
    losses, grads_down, grads_up = apply_blocks(
        hidden_all,
        lengths,
        labels,
        frozen_params,
        (down_pair, adapter_up_maps.astype(jnp.bfloat16)),
        micro_examples,
    )
    part_sums = jnp.sum(grads_down * grads_down, (1, 2, 3)) / n_head + jnp.sum(
        grads_up * grads_up, (1, 2, 3)
    )
    arrived = lax.all_to_all(
        part_sums.reshape(n_head, own_share), "head", split_axis=0, concat_axis=0, tiled=True
    )
    example_norms = jnp.sqrt(jnp.sum(arrived, 0))
    own_factor = clip_bound / jnp.maximum(example_norms, clip_bound)
    factors = lax.all_gather(own_factor, "head", axis=0, tiled=True)
    sum_down = jnp.einsum("e,eabc->abc", factors, grads_down, precision=precise)
    sum_up = jnp.einsum("e,eabc->abc", factors, grads_up, precision=precise)
    loss_part = jnp.sum(losses) / n_head
    red_down, red_up = (
        lax.psum_scatter(sum_down, "dp", scatter_dimension=1, tiled=True),
        lax.psum_scatter(sum_up, "dp", scatter_dimension=2, tiled=True),
    )
    examples = ex_dev * dataset_size
    down_gradient = (red_down + noise_mult * clip_bound * down_privacy_noise) / examples
    up_gradient = (red_up + noise_mult * clip_bound * up_privacy_noise) / examples
    step_number = optimizer_step_count.astype(jnp.float32)
    down_rows = adapter_down_maps.shape[1] // dataset_size
    down_weight = lax.dynamic_slice_in_dim(
        adapter_down_maps, lax.axis_index("dp") * down_rows, down_rows, 1
    )
    up_columns = adapter_up_maps.shape[2] // dataset_size
    up_weight = lax.dynamic_slice_in_dim(
        adapter_up_maps, lax.axis_index("dp") * up_columns, up_columns, 2
    )
    down_momentum, down_velocity, dir_down = lamb_direction(
        down_weight, down_gradient, down_first_moment, down_second_moment, step_number
    )
    up_momentum, up_velocity, dir_up = lamb_direction(
        up_weight, up_gradient, up_first_moment, up_second_moment, step_number
    )
    sq_down = (
        jnp.stack(
            [jnp.sum(down_weight * down_weight, (1, 2)), jnp.sum(dir_down * dir_down, (1, 2))], 1
        )
        / n_head
    )
    sq_up = jnp.stack([jnp.sum(up_weight * up_weight, (1, 2)), jnp.sum(dir_up * dir_up, (1, 2))], 1)
    total_down, total_up, loss_sum = lax.psum((sq_down, sq_up, loss_part), ("dp", "head"))
    norm_table = jnp.sqrt(jnp.concatenate([total_down, total_up], 0))
    updated_down = (
        down_weight - learn_rate * (norm_table[:2, 0] / norm_table[:2, 1])[:, None, None] * dir_down
    )
    updated_up = (
        up_weight - learn_rate * (norm_table[2:, 0] / norm_table[2:, 1])[:, None, None] * dir_up
    )
    return (
        loss_sum / examples,
        example_norms,
        down_momentum,
        down_velocity,
        updated_down,
        up_momentum,
        up_velocity,
        updated_up,
        norm_table,
    )


def solution(mesh):
    placed = (
        P("dp", None),
        P("dp"),
        P("dp"),
        P(),
        P("dp", "head"),
        P(),
        P(None, None, "head"),
        P("head", None),
        P(None, "head"),
        P("head", None),
        P(),
        P(),
        P(),
        P(),
        P(None, None, "head"),
        P(None, "dp", None),
        P(None, "dp", None),
        P(None, None, ("head", "dp")),
        P(None, None, ("head", "dp")),
        P(None, "dp", None),
        P(None, None, ("head", "dp")),
    )
    return jax.shard_map(
        per_device,
        mesh=mesh,
        in_specs=placed,
        out_specs=(
            P(),
            P(("dp", "head")),
            P(None, "dp", None),
            P(None, "dp", None),
            P(None, "dp", None),
            P(None, None, ("head", "dp")),
            P(None, None, ("head", "dp")),
            P(None, None, ("head", "dp")),
            P(),
        ),
        check_vma=False,
    )
```

profile of v0, /device:TPU:1, one launch (start us, length us, event | category | flops | bytes accessed | tf_op | source)
XLA Modules:
  0.0 1647.0 jit_solution(5846328891770936799)
XLA Ops:
  7.3 19.8 %all_gather.9 = s32[128,512]{1,0:T(8,128)S(1)} all-gather(s32[8,512]{1,0:T(8,128)} %param.22), channel_id=1, replica_groups=mesh['dp'=16,'head'=8] {'dp'}, dimensions={0}, use_global_device_ids=true | all-gather | bytes 278528 | tf_op jit(solution)/shard_map/all_gather | solution.py:277
  28.1 229.0 %gather_fusion = bf16[65536,128]{1,0:T(8,128)(2,1)} fusion(bf16[3144,128]{1,0:T(8,128)(2,1)S(1)} %copy-done.1, s32[65536]{0:T(1024)S(1)} %broadcast_clamp_fusion), kind=kCustom, calls=%fused_computation | custom fusion | bytes 33816576 | tf_op jit(solution)/shard_map/jit(_take)/gather | solution.py:282
  257.0 46.3 %select_convert_fusion = bf16[65536,128]{1,0:T(8,128)(2,1)} fusion(bf16[65536,128]{1,0:T(8,128)(2,1)} %gather_fusion, pred[65536]{0:T(1024)(128)(4,1)S(1)} %compare_and_fusion, pred[65536]{0:T(1024)(128)(4,1)S(1)} %bitcast.555), kind=kLoop, calls=%fused_computation.1 | loop fusion | flops 33554432 | bytes 33685504 | tf_op jit(solution)/shard_map/convert_element_type | solution.py:284
  303.4 115.6 %reduce-scatter.6.cloned.1.call-done = bf16[4096,128]{1,0:T(8,128)(2,1)} async-done(((bf16[65536,128]{1,0:T(8,128)(2,1)}), bf16[4096,128]{1,0:T(8,128)(2,1)}) %reduce-scatter.6.cloned.1.call-update) | async-done | bytes 1048592 | tf_op jit(solution)/shard_map/reduce_scatter | solution.py:283
  423.8 51.6 %all-gather.2.cloned.1.call-done = bf16[4096,1024]{1,0:T(8,128)(2,1)} async-done(((bf16[4096,128]{1,0:T(8,128)(2,1)}), bf16[4096,1024]{1,0:T(8,128)(2,1)}) %all-gather.2.cloned.1.call-update) | async-done | bytes 8388624 | tf_op jit(solution)/shard_map/all_gather | solution.py:294
  580.3 183.9 %all-reduce.15.cloned.1.call-done = (f32[1024,1024]{1,0:T(8,128)}, f32[1024,1024]{1,0:T(8,128)}, f32[1024,1024]{1,0:T(8,128)}, f32[1024,1024]{1,0:T(8,128)}) async-done(((f32[1024,1024]{1,0:T(8,128)}, f32[1024,1024]{1,0:T(8,128)}, f32[1024,1024]{1,0:T(8,128)}, f32[1024,1024]{1,0:T(8,128)}), (f32[1024,1024]{1,0:T(8,128)}, f32[1024,1024]{1,0:T(8,128)}, f32[1024,1024]{1,0:T(8,128)}, ...) | async-done | bytes 16777232 | tf_op jit(solution)/shard_map/psum | solution.py:43
  777.6 6.8 fusion.140
  806.8 6.7 fusion.137
  814.4 183.4 %all-reduce.13.cloned.1.call-done = (f32[1024,1024]{1,0:T(8,128)}, f32[1024,1024]{1,0:T(8,128)}, f32[1024,1024]{1,0:T(8,128)}, f32[1024,1024]{1,0:T(8,128)}) async-done(((f32[1024,1024]{1,0:T(8,128)}, f32[1024,1024]{1,0:T(8,128)}, f32[1024,1024]{1,0:T(8,128)}, f32[1024,1024]{1,0:T(8,128)}), (f32[1024,1024]{1,0:T(8,128)}, f32[1024,1024]{1,0:T(8,128)}, f32[1024,1024]{1,0:T(8,128)}, ...) | async-done | bytes 16777232 | tf_op jit(solution)/shard_map/psum | solution.py:43
  997.8 12.3 fusion.371
  1027.7 8.9 fusion.18
  1036.7 10.9 fusion.144
  1051.4 11.0 fusion.143
  1062.5 7.4 fusion.29
  1069.8 10.8 fusion.142
  1080.6 10.9 fusion.141
  1102.5 173.5 %all-reduce.11.cloned.1.call-done = (f32[1024,1024]{1,0:T(8,128)}, f32[1024,1024]{1,0:T(8,128)}, f32[1024,1024]{1,0:T(8,128)}, f32[1024,1024]{1,0:T(8,128)}) async-done(((f32[1024,1024]{1,0:T(8,128)}, f32[1024,1024]{1,0:T(8,128)}, f32[1024,1024]{1,0:T(8,128)}, f32[1024,1024]{1,0:T(8,128)}), (f32[1024,1024]{1,0:T(8,128)}, f32[1024,1024]{1,0:T(8,128)}, f32[1024,1024]{1,0:T(8,128)}, ...) | async-done | bytes 16777232 | tf_op jit(solution)/shard_map/psum | solution.py:146
  1276.0 7.9 fusion.370
  1359.7 29.7 %all-reduce.16 = (bf16[1024,32]{0,1:T(8,128)(2,1)}, bf16[1024,32]{0,1:T(8,128)(2,1)}, bf16[1024,32]{0,1:T(8,128)(2,1)}, bf16[1024,32]{0,1:T(8,128)(2,1)}) all-reduce(f32[1024,32]{0,1:T(8,128)S(1)} %maximum_multiply_fusion.3, f32[1024,32]{0,1:T(8,128)} %maximum_multiply_fusion.2, ...), channel_id=1, replica_groups=mesh['dp'=16,'head'=8] {'head'}, use_global_device_ids=true, to_apply=%region_73.75 | all-reduce | flops 131072 | bytes 786432 | tf_op jit(solution)/shard_map/psum | solution.py:201
  1396.8 10.8 all_to_all.6
  1409.6 12.5 all-reduce
  1426.7 64.2 %reduce-scatter.8.cloned.1.call-done = f32[2,16,8]{1,2,0:T(8,128)} async-done(((f32[2,16,128]{1,2,0:T(8,128)}), f32[2,16,8]{1,2,0:T(8,128)}) %reduce-scatter.8.cloned.1.call-update) | async-done | bytes 1040 | tf_op jit(solution)/shard_map/reduce_scatter | solution.py:331
  1492.3 74.0 %reduce-scatter.10.cloned.1.call-done = f32[64,32]{1,0:T(8,128)} async-done(((f32[1024,32]{1,0:T(8,128)}), f32[64,32]{1,0:T(8,128)}) %reduce-scatter.10.cloned.1.call-update) | async-done | bytes 8208
  1568.7 66.1 %all-reduce.1 = (f32[]{:T(128)}, f32[2,2]{0,1:T(2,128)S(1)}, f32[2,2]{0,1:T(2,128)S(1)}) all-reduce(f32[]{:T(128)S(6)} %div.320, f32[2,2]{0,1:T(2,128)S(1)} %pad_maximum_fusion.2, f32[2,2]{0,1:T(2,128)S(1)} %maximum_multiply_fusion.8), channel_id=1, replica_groups=mesh['dp'=16,'head'=8] {'dp','head'}, use_global_device_ids=true, to_apply=%region_45.47 | all-reduce | flops 9 | bytes 72 | tf_op jit(solution)/shard_map/psum | solution.py:358
  (635 shorter events, 268.8 us)
Async XLA Ops:
  7.2 770.4 %copy-start = (bf16[512,1024]{1,0:T(8,128)(2,1)S(1)}, bf16[512,1024]{1,0:T(8,128)(2,1)}, u32[]{:S(2)}) copy-start(bf16[512,1024]{1,0:T(8,128)(2,1)} %param.31) | copy-start | bytes 3145732
  7.2 20.9 %copy-start.1 = (bf16[3144,128]{1,0:T(8,128)(2,1)S(1)}, bf16[3144,128]{1,0:T(8,128)(2,1)}, u32[]{:S(2)}) copy-start(bf16[3144,128]{1,0:T(8,128)(2,1)} %param.26) | copy-start | bytes 2414596
  7.2 411.8 %reduce-scatter.6.cloned.1.call-start = ((), (), s32[]{:S(2)}) async-start(), calls=%async_computation.4 | async-start | bytes 17825792 | tf_op jit(solution)/shard_map/reduce_scatter | solution.py:283
  303.3 172.0 %all-gather.2.cloned.1.call-start = ((), (), s32[]{:S(2)}) async-start(), calls=%async_computation.5 | async-start | bytes 9437184 | tf_op jit(solution)/shard_map/all_gather | solution.py:294
  419.0 345.2 %all-reduce.15.cloned.1.call-start = ((), (), s32[]{:S(2)}) async-start(), calls=%async_computation.10 | async-start | bytes 33554432 | tf_op jit(solution)/shard_map/psum | solution.py:43
  420.7 151.7 %copy-start.88 = (bf16[2,16,128]{2,1,0:T(8,128)(2,1)}, bf16[2,16,128]{2,1,0:T(8,128)(2,1)S(1)}, u32[]{:S(2)}) copy-start(bf16[2,16,128]{2,1,0:T(8,128)(2,1)S(1)} %convert_element_type.351) | copy-start | bytes 24580
  422.0 151.4 %copy-start.111 = (pred[2,512]{1,0:T(4,128)(4,1)}, pred[2,512]{1,0:T(4,128)(4,1)S(1)}, u32[]{:S(2)}) copy-start(pred[2,512]{1,0:T(4,128)(4,1)S(1)} %get-tuple-element.137) | copy-start | bytes 3076
  500.9 19.8 %copy-start.32 = (f32[2,512,1024]{2,1,0:T(8,128)}, f32[2,512,1024]{2,1,0:T(8,128)S(1)}, u32[]{:S(2)}) copy-start(f32[2,512,1024]{2,1,0:T(8,128)S(1)} %get-tuple-element.79) | copy-start | bytes 12582916
  580.3 417.5 %all-reduce.13.cloned.1.call-start = ((), (), s32[]{:S(2)}) async-start(), calls=%async_computation.9 | async-start | bytes 33554432 | tf_op jit(solution)/shard_map/psum | solution.py:43
  813.5 462.4 %all-reduce.11.cloned.1.call-start = ((), (), s32[]{:S(2)}) async-start(), calls=%async_computation.8 | async-start | bytes 33554432 | tf_op jit(solution)/shard_map/psum | solution.py:146
  1010.1 17.6 %copy-start.4 = (f32[1024,1024]{1,0:T(8,128)}, f32[1024,1024]{1,0:T(8,128)S(1)}, u32[]{:S(2)}) copy-start(f32[1024,1024]{1,0:T(8,128)S(1)} %get-tuple-element.121) | copy-start | bytes 12582916
  1091.6 399.3 %reduce-scatter.8.cloned.1.call-start = ((), (), s32[]{:S(2)}) async-start(), calls=%async_computation.6 | async-start | bytes 139264 | tf_op jit(solution)/shard_map/reduce_scatter | solution.py:331
  1290.2 53.7 %copy-start.78 = (bf16[2,2,64,512]{3,2,1,0:T(8,128)(2,1)}, bf16[2,2,64,512]{3,2,1,0:T(8,128)(2,1)S(1)}, u32[]{:S(2)}) copy-start(bf16[2,2,64,512]{3,2,1,0:T(8,128)(2,1)S(1)} %convolution_convert_fusion) | copy-start | bytes 786436
  1307.6 40.5 %copy-start.80 = (bf16[2,2,64,512]{3,2,1,0:T(8,128)(2,1)}, bf16[2,2,64,512]{3,2,1,0:T(8,128)(2,1)S(1)}, u32[]{:S(2)}) copy-start(bf16[2,2,64,512]{3,2,1,0:T(8,128)(2,1)S(1)} %convolution_convert_fusion.1) | copy-start | bytes 786436
  1324.9 27.4 %copy-start.82 = (bf16[2,2,64,512]{3,2,1,0:T(8,128)(2,1)}, bf16[2,2,64,512]{3,2,1,0:T(8,128)(2,1)S(1)}, u32[]{:S(2)}) copy-start(bf16[2,2,64,512]{3,2,1,0:T(8,128)(2,1)S(1)} %convolution_convert_fusion.2) | copy-start | bytes 786436
  1358.9 32.7 %copy-start.38 = (bf16[2,512,1024]{2,1,0:T(8,128)(2,1)S(1)}, bf16[2,512,1024]{2,1,0:T(8,128)(2,1)}, u32[]{:S(2)}) copy-start(bf16[2,512,1024]{2,1,0:T(8,128)(2,1)} %get-tuple-element.84) | copy-start | bytes 6291460
  1423.1 143.2 %reduce-scatter.10.cloned.1.call-start = ((), (), s32[]{:S(2)}) async-start(), calls=%async_computation.7 | async-start | bytes 557056
  1423.2 67.7 %copy-start.122 = (f32[2,16,8]{1,2,0:T(8,128)S(1)}, f32[2,16,8]{1,2,0:T(8,128)}, u32[]{:S(2)}) copy-start(f32[2,16,8]{1,2,0:T(8,128)} %copy.338) | copy-start | bytes 3076
  1423.2 67.7 %copy-start.153 = (f32[2,16,8]{1,2,0:T(8,128)S(1)}, f32[2,16,8]{1,2,0:T(8,128)}, u32[]{:S(2)}) copy-start(f32[2,16,8]{1,2,0:T(8,128)} %param.42) | copy-start | bytes 3076
  1423.2 67.7 %copy-start.154 = (f32[2,16,8]{1,2,0:T(8,128)S(1)}, f32[2,16,8]{1,2,0:T(8,128)}, u32[]{:S(2)}) copy-start(f32[2,16,8]{1,2,0:T(8,128)} %param.40) | copy-start | bytes 3076
  1423.2 67.7 %copy-start.155 = (f32[2,16,8]{1,2,0:T(8,128)S(1)}, f32[2,16,8]{1,2,0:T(8,128)}, u32[]{:S(2)}) copy-start(f32[2,16,8]{1,2,0:T(8,128)} %param.39) | copy-start | bytes 3076
  1424.7 142.5 %copy-start.145 = (f32[2,64,16]{1,2,0:T(8,128)S(1)}, f32[2,64,16]{1,2,0:T(8,128)}, u32[]{:S(2)}) copy-start(f32[2,64,16]{1,2,0:T(8,128)} %param.41) | copy-start | bytes 24580
  1424.7 142.5 %copy-start.146 = (f32[2,64,16]{1,2,0:T(8,128)S(1)}, f32[2,64,16]{1,2,0:T(8,128)}, u32[]{:S(2)}) copy-start(f32[2,64,16]{1,2,0:T(8,128)} %param.38) | copy-start | bytes 24580
  1424.7 142.5 %copy-start.147 = (f32[2,64,16]{1,2,0:T(8,128)S(1)}, f32[2,64,16]{1,2,0:T(8,128)}, u32[]{:S(2)}) copy-start(f32[2,64,16]{1,2,0:T(8,128)} %param.37) | copy-start | bytes 24580
  (147 other events, 469.7 us)
Sparse Core Ops, SparseCore 0:
  303.4 115.5 reduce-scatter.5
  420.7 54.6 all-gather.1
  580.4 183.7 all-reduce.14
  813.6 184.1 all-reduce.12
  1091.7 184.2 all-reduce.10
  1423.2 67.6 reduce-scatter.7
  1494.4 71.8 reduce-scatter.9
where the time goes:
time: 1650 us
  waiting for transfers between devices  846 us (51%)
  local copies, waits for them, and re-layouts  291 us (18%)
  matrix products  177 us (11%)
  other arithmetic  169 us (10%)
  blocking collectives  139 us (8%)
  between operations  24.4 us (1%)
    psum x2, waiting for transfers between devices, branch_add(): total = lax.psum(partial_out, 'head')  367 us
    gather x1, local copies, waits for them, and re-layouts, per_device(): jnp.take(token_embedding_table, jnp.clip(ids_here, 0, vocab_local - 1), a...  229 us
    psum x1, waiting for transfers between devices, layer_forward(): d_one = d_sum_two + lax.psum(back_part, 'head')  173 us
    reduce_scatter x1, waiting for transfers between devices, per_device(): lax.psum_scatter(jnp.where(inside[:, None], picked.astype(jnp.float32), 0...  116 us
    unnamed x8, waiting for transfers between devices  74.1 us
    psum x1, blocking collectives, per_device(): lax.psum((sq_down, sq_up, loss_part), ('dp', 'head'))  66.1 us
    reduce_scatter x1, waiting for transfers between devices, per_device(): lax.psum_scatter(sum_up, 'dp', scatter_dimension=2, tiled=True)  64.2 us
    all_gather x1, waiting for transfers between devices, per_device(): tokens = lax.all_gather(columns, 'head', axis=1, tiled=True)  51.6 us
  transfers between devices with their start and end apart: 7, of which 7 were waited for; matrix products, arithmetic and copies ran while one was open for 1% of the time, Pallas kernels for 0%

commit v1 on v0

--- a/solution.py
+++ b/solution.py
@@ -2,6 +2,7 @@
 import jax.numpy as jnp
 from jax import lax
 from jax.sharding import PartitionSpec as P
+from jax.lax import axis_index, axis_size, ppermute
 
 HDIM = 64
 MICRO = 4
@@ -17,6 +18,12 @@
 learn_rate = 0.25
 norm_eps = 1e-05
 contract_last = (((1,), (1,)), ((), ()))
+
+
+def racks_drive(x0, dim_i):
+    x0 = jnp.moveaxis(x0, 0, dim_i)
+    z = x0.shape
+    return x0.reshape(*z[:dim_i], z[dim_i] * z[dim_i + 1], *z[dim_i + 2 :])
 
 
 def gelu_exact(inputs):
@@ -291,7 +298,19 @@
     down_pair = jnp.concatenate([down_reduced[0], down_reduced[1]], 1)
     micro_examples = ex_dev // MICRO
     own_share = ex_dev // n_head
-    tokens = lax.all_gather(columns, "head", axis=1, tiled=True)
+    n_dev_all = axis_size("head")
+    pieces_in = [(d, (d + 1) % n_dev_all) for d in range(n_dev_all)]
+    main, reply = ([], [])
+    series = [(no, h) for h, no in pieces_in]
+    for b in tuple(range(n_dev_all - 1)):
+        if b % 2 == 0:
+            main.append(ppermute(main[-1] if main else columns, "head", pieces_in))
+        else:
+            reply.append(ppermute(reply[-1] if reply else columns, "head", series))
+    parts_out = jnp.stack([*main[::-1], columns, *reply])
+    w_next = axis_index("head") - len(main)
+    parts_out = parts_out[(jnp.arange(n_dev_all) - w_next) % n_dev_all]
+    tokens = racks_drive(parts_out, 1)
     hidden_all, unused_std = norm_rows(
         tokens.astype(jnp.float32).reshape(ex_dev, sequence_length, width) + pos_f,
         layer_norm_gains[0],

time: 1650 us -> 1740 us (1.055)
  local copies, waits for them, and re-layouts: 291 us -> 360 us
  other arithmetic: 169 us -> 190 us
    all_gather x1 -> x0, waiting for transfers between devices: 51.6 us -> none  [per_device(): tokens = lax.all_gather(columns, 'head', axis=1, tiled=True)]
    convert_element_type x0 -> x2, local copies, waits for them, and re-layouts: none -> 36 us  [per_device(): tokens.astype(jnp.float32).reshape(ex_dev, sequence_length, width) + pos_f]
    ppermute x0 -> x7, waiting for transfers between devices: none -> 34.8 us  [the longest x4 34.4 us: per_device(): main.append(ppermute(main[-1] if main else columns, 'head', pieces_in))]
    unnamed x358 -> x380, local copies, waits for them, and re-layouts: 30.4 us -> 53.3 us
    unnamed x8 -> x7, waiting for transfers between devices: 74.1 us -> 74 us
  transfers between devices with their start and end apart: 7 -> 13, of which waited for: 7 -> 10; matrix products, arithmetic and copies ran while one was open for 1% -> 2% of each run, Pallas kernels for 0% -> 0%
where the time goes in v1:
time: 1740 us; the launch traced here: 1730 us
  waiting for transfers between devices  830 us (48%)
  local copies, waits for them, and re-layouts  360 us (21%)
  other arithmetic  190 us (11%)
  matrix products  178 us (10%)
  blocking collectives  139 us (8%)
  between operations  24.5 us (1%)
    psum x2, waiting for transfers between devices, branch_add(): total = lax.psum(partial_out, 'head')  368 us
    gather x1, local copies, waits for them, and re-layouts, per_device(): jnp.take(token_embedding_table, jnp.clip(ids_here, 0, vocab_local - 1), a...  227 us
    psum x1, waiting for transfers between devices, layer_forward(): d_one = d_sum_two + lax.psum(back_part, 'head')  173 us
    reduce_scatter x1, waiting for transfers between devices, per_device(): lax.psum_scatter(jnp.where(inside[:, None], picked.astype(jnp.float32), 0...  116 us
    unnamed x7, waiting for transfers between devices  74 us
    psum x1, blocking collectives, per_device(): lax.psum((sq_down, sq_up, loss_part), ('dp', 'head'))  66 us
    reduce_scatter x1, waiting for transfers between devices, per_device(): lax.psum_scatter(sum_up, 'dp', scatter_dimension=2, tiled=True)  64.1 us
    unnamed x380, local copies, waits for them, and re-layouts  53.3 us
  transfers between devices with their start and end apart: 13, of which 10 were waited for; matrix products, arithmetic and copies ran while one was open for 2% of the time, Pallas kernels for 0%

profile of v1, /device:TPU:1, one launch (start us, length us, event | category | flops | bytes accessed | tf_op | source)
XLA Modules:
  0.0 1734.5 jit_solution(10301829808593857820)
XLA Ops:
  7.3 19.8 %all_gather.6 = s32[128,512]{1,0:T(8,128)S(1)} all-gather(s32[8,512]{1,0:T(8,128)} %param.22), channel_id=1, replica_groups=mesh['dp'=16,'head'=8] {'dp'}, dimensions={0}, use_global_device_ids=true | all-gather | bytes 278528 | tf_op jit(solution)/shard_map/all_gather | solution.py:284
  28.1 227.3 %gather_fusion = bf16[65536,128]{1,0:T(8,128)(2,1)} fusion(bf16[3144,128]{1,0:T(8,128)(2,1)S(1)} %copy-done.1, s32[65536]{0:T(1024)S(1)} %broadcast_clamp_fusion), kind=kCustom, calls=%fused_computation | custom fusion | bytes 33816576 | tf_op jit(solution)/shard_map/jit(_take)/gather | solution.py:289
  255.3 46.3 %select_convert_fusion = bf16[65536,128]{1,0:T(8,128)(2,1)} fusion(bf16[65536,128]{1,0:T(8,128)(2,1)} %gather_fusion, pred[65536]{0:T(1024)(128)(4,1)S(1)} %compare_and_fusion, pred[65536]{0:T(1024)(128)(4,1)S(1)} %bitcast.578), kind=kLoop, calls=%fused_computation.2 | loop fusion | flops 33554432 | bytes 33685504 | tf_op jit(solution)/shard_map/convert_element_type | solution.py:291
  301.7 115.7 %reduce-scatter.6.cloned.1.call-done = bf16[4096,128]{1,0:T(8,128)(2,1)} async-done(((bf16[65536,128]{1,0:T(8,128)(2,1)}), bf16[4096,128]{1,0:T(8,128)(2,1)}) %reduce-scatter.6.cloned.1.call-update) | async-done | bytes 1048592 | tf_op jit(solution)/shard_map/reduce_scatter | solution.py:290
  419.6 12.1 collective-permute-done
  435.1 11.6 collective-permute-done.1
  450.8 10.7 collective-permute-done.2
  514.4 11.5 fusion
  535.6 17.8 %copy.184 = f32[4096,8,128]{2,1,0:T(8,128)} copy(f32[4096,8,128]{2,0,1:T(8,128)} %convert_bitcast_fusion) | data formatting | bytes 33554432 | tf_op jit(solution)/shard_map/convert_element_type | solution.py:315
  553.4 18.2 %reshape.710 = f32[8,512,1024]{2,1,0:T(8,128)} reshape(f32[4096,8,128]{2,1,0:T(8,128)} %copy.184) | data formatting | bytes 33554432 | tf_op jit(solution)/shard_map/convert_element_type | solution.py:315
  667.6 184.2 %all-reduce.15.cloned.1.call-done = (f32[1024,1024]{1,0:T(8,128)}, f32[1024,1024]{1,0:T(8,128)}, f32[1024,1024]{1,0:T(8,128)}, f32[1024,1024]{1,0:T(8,128)}) async-done(((f32[1024,1024]{1,0:T(8,128)}, f32[1024,1024]{1,0:T(8,128)}, f32[1024,1024]{1,0:T(8,128)}, f32[1024,1024]{1,0:T(8,128)}), (f32[1024,1024]{1,0:T(8,128)}, f32[1024,1024]{1,0:T(8,128)}, f32[1024,1024]{1,0:T(8,128)}, ...) | async-done | bytes 16777232 | tf_op jit(solution)/shard_map/psum | solution.py:50
  902.1 183.4 %all-reduce.13.cloned.1.call-done = (f32[1024,1024]{1,0:T(8,128)}, f32[1024,1024]{1,0:T(8,128)}, f32[1024,1024]{1,0:T(8,128)}, f32[1024,1024]{1,0:T(8,128)}) async-done(((f32[1024,1024]{1,0:T(8,128)}, f32[1024,1024]{1,0:T(8,128)}, f32[1024,1024]{1,0:T(8,128)}, f32[1024,1024]{1,0:T(8,128)}), (f32[1024,1024]{1,0:T(8,128)}, f32[1024,1024]{1,0:T(8,128)}, f32[1024,1024]{1,0:T(8,128)}, ...) | async-done | bytes 16777232 | tf_op jit(solution)/shard_map/psum | solution.py:50
  1085.5 12.5 fusion.373
  1124.3 10.9 fusion.144
  1139.1 11.0 fusion.143
  1157.5 11.0 fusion.142
  1168.5 10.8 fusion.141
  1190.3 173.4 %all-reduce.11.cloned.1.call-done = (f32[1024,1024]{1,0:T(8,128)}, f32[1024,1024]{1,0:T(8,128)}, f32[1024,1024]{1,0:T(8,128)}, f32[1024,1024]{1,0:T(8,128)}) async-done(((f32[1024,1024]{1,0:T(8,128)}, f32[1024,1024]{1,0:T(8,128)}, f32[1024,1024]{1,0:T(8,128)}, f32[1024,1024]{1,0:T(8,128)}), (f32[1024,1024]{1,0:T(8,128)}, f32[1024,1024]{1,0:T(8,128)}, f32[1024,1024]{1,0:T(8,128)}, ...) | async-done | bytes 16777232 | tf_op jit(solution)/shard_map/psum | solution.py:153
  1447.3 29.8 %all-reduce.16 = (bf16[1024,32]{0,1:T(8,128)(2,1)}, bf16[1024,32]{0,1:T(8,128)(2,1)}, bf16[1024,32]{0,1:T(8,128)(2,1)}, bf16[1024,32]{0,1:T(8,128)(2,1)}) all-reduce(f32[1024,32]{0,1:T(8,128)S(1)} %maximum_multiply_fusion.3, f32[1024,32]{0,1:T(8,128)} %maximum_multiply_fusion.2, ...), channel_id=1, replica_groups=mesh['dp'=16,'head'=8] {'head'}, use_global_device_ids=true, to_apply=%region_73.75 | all-reduce | flops 131072 | bytes 786432 | tf_op jit(solution)/shard_map/psum | solution.py:208
  1484.4 10.8 all_to_all.6
  1497.3 12.5 all-reduce
  1514.4 64.1 %reduce-scatter.8.cloned.1.call-done = f32[2,16,8]{1,2,0:T(8,128)} async-done(((f32[2,16,128]{1,2,0:T(8,128)}), f32[2,16,8]{1,2,0:T(8,128)}) %reduce-scatter.8.cloned.1.call-update) | async-done | bytes 1040 | tf_op jit(solution)/shard_map/reduce_scatter | solution.py:350
  1579.9 73.9 %reduce-scatter.10.cloned.1.call-done = f32[64,32]{1,0:T(8,128)} async-done(((f32[1024,32]{1,0:T(8,128)}), f32[64,32]{1,0:T(8,128)}) %reduce-scatter.10.cloned.1.call-update) | async-done | bytes 8208
  1656.2 66.0 %all-reduce.1 = (f32[]{:T(128)}, f32[2,2]{0,1:T(2,128)S(1)}, f32[2,2]{0,1:T(2,128)S(1)}) all-reduce(f32[]{:T(128)S(6)} %div.320, f32[2,2]{0,1:T(2,128)S(1)} %pad_maximum_fusion.2, f32[2,2]{0,1:T(2,128)S(1)} %maximum_multiply_fusion.8), channel_id=1, replica_groups=mesh['dp'=16,'head'=8] {'dp','head'}, use_global_device_ids=true, to_apply=%region_45.47 | all-reduce | flops 9 | bytes 72 | tf_op jit(solution)/shard_map/psum | solution.py:377
  (677 shorter events, 364.8 us)
Async XLA Ops:
  7.2 858.0 %copy-start = (bf16[512,1024]{1,0:T(8,128)(2,1)S(1)}, bf16[512,1024]{1,0:T(8,128)(2,1)}, u32[]{:S(2)}) copy-start(bf16[512,1024]{1,0:T(8,128)(2,1)} %param.31) | copy-start | bytes 3145732
  7.2 410.2 %reduce-scatter.6.cloned.1.call-start = ((), (), s32[]{:S(2)}) async-start(), calls=%async_computation.4 | async-start | bytes 17825792 | tf_op jit(solution)/shard_map/reduce_scatter | solution.py:290
  301.6 147.8 %copy-start.153 = (s32[8]{0:T(128)S(1)}, s32[8]{0:T(128)}, u32[]{:S(2)}) copy-start(s32[8]{0:T(128)} %param.23) | copy-start | bytes 100
  301.6 162.3 %copy-start.45 = (bf16[512,1024]{1,0:T(8,128)(2,1)S(1)}, bf16[512,1024]{1,0:T(8,128)(2,1)}, u32[]{:S(2)}) copy-start(bf16[512,1024]{1,0:T(8,128)(2,1)} %param.27) | copy-start | bytes 3145732
  301.6 550.2 %all-reduce.15.cloned.1.call-start = ((), (), s32[]{:S(2)}) async-start(), calls=%async_computation.9 | async-start | bytes 33554432 | tf_op jit(solution)/shard_map/psum | solution.py:50
  417.4 14.3 collective-permute-start
  432.7 14.1 collective-permute-start.1
  435.0 14.8 collective-permute-start.4
  446.8 14.6 collective-permute-start.2
  449.9 28.7 %collective-permute-start.5 = (bf16[4096,128]{1,0:T(8,128)(2,1)}, bf16[4096,128]{1,0:T(8,128)(2,1)}, u32[]{:S(2)}, u32[]{:S(2)}) collective-permute-start(bf16[4096,128]{1,0:T(8,128)(2,1)} %collective-permute-done.4), channel_id=1, source_target_pairs={{1,0},{2,1},{3,2},{4,3},{5,4},{6,5},{7,6},{0,7},{9,8},{10,9},{11,1... | collective-permute-start | bytes 3145736 | tf_op jit(solution)/shard_map/ppermute | solution.py:309
  461.4 19.6 %collective-permute-start.3 = (bf16[4096,128]{1,0:T(8,128)(2,1)}, bf16[4096,128]{1,0:T(8,128)(2,1)}, u32[]{:S(2)}, u32[]{:S(2)}) collective-permute-start(bf16[4096,128]{1,0:T(8,128)(2,1)} %collective-permute-done.2), channel_id=1, source_target_pairs={{0,1},{1,2},{2,3},{3,4},{4,5},{5,6},{6,7},{7,0},{8,9},{9,10},{10,1... | collective-permute-start | bytes 3145736 | tf_op jit(solution)/shard_map/ppermute | solution.py:307
  476.1 183.6 %copy-start.93 = (bf16[2,16,128]{2,1,0:T(8,128)(2,1)}, bf16[2,16,128]{2,1,0:T(8,128)(2,1)S(1)}, u32[]{:S(2)}) copy-start(bf16[2,16,128]{2,1,0:T(8,128)(2,1)S(1)} %convert_element_type.366) | copy-start | bytes 24580
  476.7 183.9 %copy-start.116 = (pred[2,512]{1,0:T(4,128)(4,1)}, pred[2,512]{1,0:T(4,128)(4,1)S(1)}, u32[]{:S(2)}) copy-start(pred[2,512]{1,0:T(4,128)(4,1)S(1)} %get-tuple-element.137) | copy-start | bytes 3076
  478.5 16.2 collective-permute-start.6
  667.6 417.9 %all-reduce.13.cloned.1.call-start = ((), (), s32[]{:S(2)}) async-start(), calls=%async_computation.8 | async-start | bytes 33554432 | tf_op jit(solution)/shard_map/psum | solution.py:50
  901.2 462.6 %all-reduce.11.cloned.1.call-start = ((), (), s32[]{:S(2)}) async-start(), calls=%async_computation.7 | async-start | bytes 33554432 | tf_op jit(solution)/shard_map/psum | solution.py:153
  1179.4 399.1 %reduce-scatter.8.cloned.1.call-start = ((), (), s32[]{:S(2)}) async-start(), calls=%async_computation.5 | async-start | bytes 139264 | tf_op jit(solution)/shard_map/reduce_scatter | solution.py:350
  1510.8 143.0 %reduce-scatter.10.cloned.1.call-start = ((), (), s32[]{:S(2)}) async-start(), calls=%async_computation.6 | async-start | bytes 557056
  1510.8 67.7 %copy-start.127 = (f32[2,16,8]{1,2,0:T(8,128)S(1)}, f32[2,16,8]{1,2,0:T(8,128)}, u32[]{:S(2)}) copy-start(f32[2,16,8]{1,2,0:T(8,128)} %copy.344) | copy-start | bytes 3076
  1510.8 67.7 %copy-start.158 = (f32[2,16,8]{1,2,0:T(8,128)S(1)}, f32[2,16,8]{1,2,0:T(8,128)}, u32[]{:S(2)}) copy-start(f32[2,16,8]{1,2,0:T(8,128)} %param.42) | copy-start | bytes 3076
  1510.8 67.7 %copy-start.159 = (f32[2,16,8]{1,2,0:T(8,128)S(1)}, f32[2,16,8]{1,2,0:T(8,128)}, u32[]{:S(2)}) copy-start(f32[2,16,8]{1,2,0:T(8,128)} %param.40) | copy-start | bytes 3076
  1512.4 142.4 %copy-start.150 = (f32[2,64,16]{1,2,0:T(8,128)S(1)}, f32[2,64,16]{1,2,0:T(8,128)}, u32[]{:S(2)}) copy-start(f32[2,64,16]{1,2,0:T(8,128)} %param.41) | copy-start | bytes 24580
  1512.4 142.4 %copy-start.151 = (f32[2,64,16]{1,2,0:T(8,128)S(1)}, f32[2,64,16]{1,2,0:T(8,128)}, u32[]{:S(2)}) copy-start(f32[2,64,16]{1,2,0:T(8,128)} %param.38) | copy-start | bytes 24580
  1512.4 142.3 %copy-start.152 = (f32[2,64,16]{1,2,0:T(8,128)S(1)}, f32[2,64,16]{1,2,0:T(8,128)}, u32[]{:S(2)}) copy-start(f32[2,64,16]{1,2,0:T(8,128)} %param.37) | copy-start | bytes 24580
  (160 other events, 861.1 us)
Sparse Core Ops, SparseCore 0:
  301.8 115.5 reduce-scatter.5
  667.7 184.1 all-reduce.14
  901.3 184.1 all-reduce.12
  1179.5 184.1 all-reduce.10
  1510.9 67.5 reduce-scatter.7
  1581.9 71.8 reduce-scatter.9
